TPU v7x, 512 devices: a whole 4x4x16 slice. The times are simulated.
512 devices in a mesh: kv: 8 (over x, core), pool: 64 (over y, z).
Axes of the slice: x: 4, y: 4, z: 16, core: 2. Of those that a mesh axis runs over, the one named last changes fastest.
Arguments:
- hidden: bfloat16 [64, 2048], P('pool'), may hold values from -6 to 6
- norm_attn: bfloat16 [2048], replicated, may hold values from 0.099609375 to 1.8984375
- wq: bfloat16 [2048, 2048], P(None, 'kv'), may hold values from -0.125 to 0.125
- wkv: bfloat16 [2, 2048, 1024], P(None, None, 'kv'), may hold values from -0.125 to 0.125
- wo: bfloat16 [2048, 2048], P('kv'), may hold values from -0.125 to 0.125
- cache: bfloat16 [2, 1024, 128, 1024], P(None, 'pool', None, 'kv'), may hold values from -70 to 70, as said below
- slot_entry: int32 [1024], P('pool'), may hold values from -1 to 4095, as said below
- lengths: int32 [64], replicated, may hold values from 1 to 8192, as said below
- norm_mlp: bfloat16 [2048], replicated, may hold values from 0.099609375 to 1.8984375
- w_gate: bfloat16 [2048, 8192], P('pool', 'kv'), may hold values from -0.125 to 0.125
- w_up: bfloat16 [2048, 8192], P('pool', 'kv'), may hold values from -0.125 to 0.125
- w_down: bfloat16 [8192, 2048], P('kv', 'pool'), may hold values from -0.0625 to 0.0625
Outputs:
- output: bfloat16 [64, 2048], P('pool')
Inputs may be any that keep to these rules, and one draw needn't show every extreme that they name: slot_entry[s] is -1 for a free slot, else r * 64 + b: the slot holds block b of request r, that is its cached positions b * 128 to b * 128 + 127 that lie below lengths[r]. Every block of every request below ceil(lengths[r] / 128) sits in exactly one slot, anywhere in the pool; a holder's slots are its 16 entries. Its new token stands at position lengths[r]. `cache`: keys and values of the cached tokens, already rotated.
All inputs are finite; a program needn't handle non-finite values.
Results may differ from a plain program's by a relative error of at most 0.012.
The roundings to bfloat16 on the way count: a program that leaves them out, or rounds other values in their place, can miss the bound.
Values may be sent and summed in bfloat16 or wider, within the bound.
A program may use at most 64 MiB of HBM per device.

v0:
```python
import math
import jax
import jax.numpy as jnp
from jax import lax
from jax.sharding import PartitionSpec as P

QUERY_HEAD_COUNT = 16
KEY_VALUE_HEADS = 8
HEAD_SIZE = 128
NEGATIVE = -1e30
EPSILON = 1e-05
ROPE_BASE = 1000000.0


def combined_all(x, axis, combine):
    everything = jax.tree.map(lambda part: lax.all_gather(part, axis), x)
    initial = jax.tree.map(lambda part: part[0], everything)

    def step(k, so_far):
        return combine(so_far, jax.tree.map(lambda part: part[k], everything))

    return lax.fori_loop(1, lax.axis_size(axis), step, initial)


def narrow_rows(tensor):
    return lax.optimization_barrier(tensor.astype(jnp.bfloat16))


def rms_scale(inputs, gain_vec):
    widened = inputs.astype(jnp.float32)
    mean_square = jnp.mean(widened * widened, axis=-1, keepdims=True)
    return narrow_rows(widened * lax.rsqrt(mean_square + EPSILON) * gain_vec.astype(jnp.float32))


def rotate(vectors, positions):
    head_width = vectors.shape[-1]
    halfway = head_width // 2
    frequency = jnp.exp(
        jnp.arange(halfway, dtype=jnp.float32) * (-2.0 * math.log(ROPE_BASE) / head_width)
    )
    angles = positions.astype(jnp.float32)[:, None] * frequency[None, :]
    cosine = jnp.cos(angles)[:, None, :]
    sine_of = jnp.sin(angles)[:, None, :]
    leading = vectors[..., :halfway]
    trailing = vectors[..., halfway:]
    return jnp.concatenate(
        [leading * cosine - trailing * sine_of, trailing * cosine + leading * sine_of], axis=-1
    )


def combine(earlier, latter):
    highest = jnp.maximum(earlier[0], latter[0])
    scale_early = jnp.exp(earlier[0] - highest)
    scale_late = jnp.exp(latter[0] - highest)
    row_count, head_count = highest.shape
    feature = earlier[2].shape[1] // head_count
    early_out = earlier[2].reshape(row_count, head_count, feature) * scale_early[:, :, None]
    late_out = latter[2].reshape(row_count, head_count, feature) * scale_late[:, :, None]
    weight_sum = earlier[1] * scale_early + latter[1] * scale_late
    return (highest, weight_sum, (early_out + late_out).reshape(row_count, head_count * feature))


def per_device(
    hidden, norm_attn, wq, wkv, wo, cache, slot_entry, lengths, norm_mlp, w_gate, w_up, w_down
):
    home_rows = hidden.shape[0]
    shared_heads = wkv.shape[2] // HEAD_SIZE
    queries_per_shared = QUERY_HEAD_COUNT // KEY_VALUE_HEADS
    query_heads = shared_heads * queries_per_shared
    home_index = lax.axis_index("pool")
    max_blocks = slot_entry.shape[0] * lax.axis_size("pool") // 16
    positions = lax.dynamic_slice_in_dim(lengths, home_index * home_rows, home_rows)
    normed_input = rms_scale(hidden, norm_attn)
    query_rows = jnp.dot(normed_input, wq, preferred_element_type=jnp.float32).reshape(
        home_rows, query_heads, HEAD_SIZE
    )
    query_rows = narrow_rows(rotate(query_rows, positions) * HEAD_SIZE ** (-0.5))
    fresh_keys = jnp.dot(normed_input, wkv[0], preferred_element_type=jnp.float32).reshape(
        home_rows, shared_heads, HEAD_SIZE
    )
    fresh_keys = narrow_rows(rotate(fresh_keys, positions))
    fresh_values = narrow_rows(
        jnp.dot(normed_input, wkv[1], preferred_element_type=jnp.float32)
    ).reshape(home_rows, shared_heads, HEAD_SIZE)
    every_query = lax.all_gather(
        query_rows.reshape(home_rows, query_heads * HEAD_SIZE), "pool", axis=0, tiled=True
    )
    request_list = every_query.shape[0]
    every_query = every_query.reshape(request_list, shared_heads, queries_per_shared, HEAD_SIZE)
    slot_count = slot_entry.shape[0]
    block_len = cache.shape[2]
    live_slot = slot_entry >= 0
    owners = jnp.where(live_slot, slot_entry // max_blocks, 0)
    block_index = jnp.where(live_slot, slot_entry % max_blocks, 0)
    picked = every_query[owners]
    block_keys = cache[0].reshape(slot_count, block_len, shared_heads, HEAD_SIZE)
    block_values = cache[1].reshape(slot_count, block_len, shared_heads, HEAD_SIZE)
    scores = jnp.einsum("sgjd,stgd->sgjt", picked, block_keys, preferred_element_type=jnp.float32)
    position = block_index[:, None] * block_len + jnp.arange(block_len, dtype=jnp.int32)[None, :]
    in_range = live_slot[:, None] & (position < lengths[owners][:, None])
    scores = jnp.where(in_range[:, None, None, :], scores, NEGATIVE)
    block_max = jnp.max(scores, axis=-1)
    same_owner = (owners[:, None] == owners[None, :]) & live_slot[:, None] & live_slot[None, :]
    holder_max = jnp.max(jnp.where(same_owner[:, :, None, None], block_max[None], NEGATIVE), axis=1)
    raised = jnp.where(in_range[:, None, None, :], jnp.exp(scores - holder_max[..., None]), 0.0)
    holder_total = jnp.sum(raised, axis=-1)
    holder_output = jnp.einsum(
        "sgjt,stgd->sgjd", narrow_rows(raised), block_values, preferred_element_type=jnp.float32
    )
    member = (owners[:, None] == jnp.arange(request_list, dtype=jnp.int32)[None, :]) & live_slot[
        :, None
    ]
    request_max = jnp.max(jnp.where(member.T[:, :, None, None], holder_max[None], NEGATIVE), axis=1)
    request_max = request_max.reshape(request_list, query_heads)
    member_float = member.astype(jnp.float32)
    request_total = jnp.einsum(
        "sr,sgj->rgj", member_float, holder_total, precision=lax.Precision.HIGHEST
    )
    request_total = request_total.reshape(request_list, query_heads)
    request_out = jnp.einsum(
        "sr,sgjd->rgjd", member_float, holder_output, precision=lax.Precision.HIGHEST
    )
    request_out = request_out.reshape(request_list, query_heads * HEAD_SIZE)
    merged = combined_all((request_max, request_total, request_out), "pool", combine)
    part_max = lax.dynamic_slice_in_dim(merged[0], home_index * home_rows, home_rows)
    part_total = lax.dynamic_slice_in_dim(merged[1], home_index * home_rows, home_rows)
    part_out = lax.dynamic_slice_in_dim(merged[2], home_index * home_rows, home_rows)
    own_query = query_rows.reshape(home_rows, shared_heads, queries_per_shared, HEAD_SIZE).astype(
        jnp.float32
    )
    new_score = jnp.sum(own_query * fresh_keys.astype(jnp.float32)[:, :, None, :], axis=-1).reshape(
        home_rows, query_heads
    )
    highest = jnp.maximum(part_max, new_score)
    old_scale = jnp.exp(part_max - highest)
    new_scale = jnp.exp(new_score - highest)
    weight_sum = part_total * old_scale + new_scale
    new_term = (
        new_scale.reshape(home_rows, shared_heads, queries_per_shared)[..., None]
        * fresh_values.astype(jnp.float32)[:, :, None, :]
    )
    combined = part_out.reshape(home_rows, query_heads, HEAD_SIZE) * old_scale[
        ..., None
    ] + new_term.reshape(home_rows, query_heads, HEAD_SIZE)
    attended = narrow_rows(combined / weight_sum[..., None]).reshape(
        home_rows, query_heads * HEAD_SIZE
    )
    projected = lax.psum(jnp.dot(attended, wo, preferred_element_type=jnp.float32), "kv")
    residual = narrow_rows(hidden.astype(jnp.float32) + projected)
    mlp_in = rms_scale(residual, norm_mlp)
    columns = lax.all_to_all(mlp_in, "pool", split_axis=1, concat_axis=0, tiled=True)
    hidden_width = w_gate.shape[1]
    gate_term = jnp.dot(columns, w_gate, preferred_element_type=jnp.float32)
    up_term = jnp.dot(columns, w_up, preferred_element_type=jnp.float32)
    summed = lax.psum_scatter(
        jnp.concatenate([gate_term, up_term], axis=1), "pool", scatter_dimension=0, tiled=True
    )
    activation = narrow_rows(jax.nn.silu(summed[:, :hidden_width]) * summed[:, hidden_width:])
    projected_down = jnp.dot(
        lax.all_gather(activation, "pool", axis=0, tiled=True),
        w_down,
        preferred_element_type=jnp.float32,
    )
    mlp_out = narrow_rows(lax.psum(projected_down, "kv"))
    returned = lax.all_to_all(mlp_out, "pool", split_axis=0, concat_axis=1, tiled=True)
    return (residual.astype(jnp.float32) + returned.astype(jnp.float32)).astype(jnp.bfloat16)


def solution(mesh):
    return jax.shard_map(
        per_device,
        mesh=mesh,
        in_specs=(
            P("pool", None),
            P(),
            P(None, "kv"),
            P(None, None, "kv"),
            P("kv", None),
            P(None, "pool", None, "kv"),
            P("pool"),
            P(),
            P(),
            P("pool", "kv"),
            P("pool", "kv"),
            P("kv", "pool"),
        ),
        out_specs=P("pool", None),
        check_vma=False,
    )
```

profile of v0, /device:TPU:8, one launch (start us, length us, event | category | flops | bytes accessed | tf_op | source)
XLA Modules:
  0.0 794.5 jit_solution(5610471597167837660)
XLA Ops:
  8.0 1.2 dynamic_slice.42
  10.6 1.3 multiply_reduce_fusion.1
  13.3 1.5 fusion.5
  15.0 88.2 %all-gather.3 = bf16[64,1,256]{2,1,0:T(2,128)(2,1)S(1)} all-gather(bf16[1,1,256]{2,1,0:T(2,128)(2,1)S(1)} %reshape.618), channel_id=1, replica_groups=mesh['kv'=8,'pool'=64] {'pool'}, dimensions={0}, use_global_device_ids=true | all-gather | bytes 33280 | tf_op jit(solution)/shard_map/all_gather | solution.py:85
  103.4 1.3 gather_fusion
  105.5 1.5 fusion.61
  107.5 1.3 fusion.10
  108.8 0.9 fusion.20
  109.8 1.2 convolution_bitcast_fusion.2
  111.2 1.2 fusion.4
  112.6 79.4 %all-gather.5 = f32[64,64,2]{1,2,0:T(2,128)S(1)} all-gather(f32[1,64,2]{1,2,0:T(2,128)S(1)} %convolution_bitcast_fusion), channel_id=3, replica_groups=mesh['kv'=8,'pool'=64] {'pool'}, dimensions={0}, use_global_device_ids=true | all-gather | bytes 33280 | tf_op jit(solution)/shard_map/all_gather | solution.py:16
  192.2 81.0 %all-gather.4 = f32[64,64,2]{1,2,0:T(2,128)S(1)} all-gather(f32[1,64,2]{1,2,0:T(2,128)S(1)} %bitcast.156), channel_id=2, replica_groups=mesh['kv'=8,'pool'=64] {'pool'}, dimensions={0}, use_global_device_ids=true | all-gather | bytes 33280 | tf_op jit(solution)/shard_map/all_gather | solution.py:16
  274.2 87.2 %while.19 = (s32[]{:T(128)}, f32[64,2]{0,1:T(2,128)S(1)}, f32[64,2]{0,1:T(2,128)S(1)}, f32[64,256]{1,0:T(8,128)S(1)}, f32[64,64,2]{1,2,0:T(2,128)S(1)}, /*index=...) while((s32[]{:T(128)}, f32[64,2]{0,1:T(2,128)S(1)}, ...), condition=%wide.region_6.7_spmd, body=%wide.region_5.6_spmd.sunk | while | flops 49925 | bytes 466071 | solution.py:22
  274.7 0.9 fusion.74
  280.2 0.9 fusion.74
  281.6 0.9 fusion.74
  283.0 0.9 fusion.74
  284.4 0.9 fusion.74
  288.5 0.9 fusion.74
  289.9 0.9 fusion.74
  291.3 0.9 fusion.74
  292.7 0.9 fusion.74
  298.2 0.9 fusion.74
  299.6 0.9 fusion.74
  362.0 12.6 %psum.14 = f32[1,2048]{1,0:T(1,128)S(1)} all-reduce(f32[1,2048]{1,0:T(1,128)S(1)} %fusion.62), channel_id=1, replica_groups=mesh['kv'=8,'pool'=64] {'kv'}, use_global_device_ids=true, to_apply=%region_8.9 | all-reduce | flops 2048 | bytes 16384 | tf_op jit(solution)/shard_map/psum | solution.py:148
  376.2 23.6 %all_to_all.30 = bf16[1,64,32]{2,0,1:T(2,128)(2,1)S(1)} all-to-all(bf16[1,64,32]{2,0,1:T(2,128)(2,1)S(1)} %all_to_all.27), channel_id=1, replica_groups=mesh['kv'=8,'pool'=64] {'pool'}, dimensions={1} | all-to-all | bytes 8192 | tf_op jit(solution)/shard_map/all_to_all | solution.py:151
  401.1 1.3 dynamic-slice
  402.4 255.3 %all-reduce.3.cloned.1.call-done = f32[64,2048]{1,0:T(8,128)} async-done(((f32[64,2048]{1,0:T(8,128)}), f32[64,2048]{1,0:T(8,128)}) %all-reduce.3.cloned.1.call-update) | async-done | bytes 524304
  657.7 1.5 fusion.39
  659.2 80.6 %all-gather.6 = bf16[64,1,1024]{2,1,0:T(2,128)(2,1)S(1)} all-gather(bf16[1,1,1024]{2,1,0:T(2,128)(2,1)S(1)} %bitcast.153), channel_id=1, replica_groups=mesh['kv'=8,'pool'=64] {'pool'}, dimensions={0}, use_global_device_ids=true | all-gather | bytes 133120 | tf_op jit(solution)/shard_map/all_gather | solution.py:160
  739.9 23.6 %psum.15 = bf16[64,32]{0,1:T(8,128)(2,1)S(1)} all-reduce(f32[64,32]{0,1:T(8,128)S(1)} %fusion.17), channel_id=1, replica_groups=mesh['kv'=8,'pool'=64] {'kv'}, use_global_device_ids=true, to_apply=%region_11.12 | all-reduce | flops 2048 | bytes 12288 | tf_op jit(solution)/shard_map/psum | solution.py:164
  763.5 23.4 %all_to_all.31 = bf16[64,1,32]{2,1,0:T(2,128)(2,1)S(1)} all-to-all(bf16[64,1,32]{2,1,0:T(2,128)(2,1)S(1)} %copy.51), channel_id=1, replica_groups=mesh['kv'=8,'pool'=64] {'pool'}, dimensions={0} | all-to-all | bytes 8192 | tf_op jit(solution)/shard_map/all_to_all | solution.py:165
  (435 shorter events, 84.9 us)
Async XLA Ops:
  6.5 355.2 %copy-start = (bf16[256,2048]{1,0:T(8,128)(2,1)S(1)}, bf16[256,2048]{1,0:T(8,128)(2,1)}, u32[]{:S(2)}) copy-start(bf16[256,2048]{1,0:T(8,128)(2,1)} %param.18) | copy-start | bytes 3145732
  6.5 105.9 %copy-start.4 = (bf16[2048]{0:T(1024)(128)(2,1)S(1)}, bf16[2048]{0:T(1024)(128)(2,1)}, u32[]{:S(2)}) copy-start(bf16[2048]{0:T(1024)(128)(2,1)} %param.22) | copy-start | bytes 12292
  6.5 266.8 %all-gather.9.cloned.1.call-start = ((), (), s32[]{:S(2)}) async-start(), calls=%async_computation.2 | async-start | bytes 4259840 | tf_op jit(solution)/shard_map/all_gather | solution.py:16
  14.8 359.9 %copy-start.1 = (bf16[1,2048]{1,0:T(2,128)(2,1)S(1)}, bf16[1,2048]{1,0:T(2,128)(2,1)}, u32[]{:S(2)}) copy-start(bf16[1,2048]{1,0:T(2,128)(2,1)} %param.14) | copy-start | bytes 12292
  15.0 384.8 %copy-start.2 = (bf16[32,1024]{1,0:T(8,128)(2,1)S(1)}, bf16[32,1024]{1,0:T(8,128)(2,1)}, u32[]{:S(2)}) copy-start(bf16[32,1024]{1,0:T(8,128)(2,1)} %param.24) | copy-start | bytes 196612
  103.4 296.6 %copy-start.3 = (bf16[32,1024]{1,0:T(8,128)(2,1)S(1)}, bf16[32,1024]{1,0:T(8,128)(2,1)}, u32[]{:S(2)}) copy-start(bf16[32,1024]{1,0:T(8,128)(2,1)} %param.23) | copy-start | bytes 196612
  109.7 547.9 %all-reduce.3.cloned.1.call-start = ((), (), s32[]{:S(2)}) async-start(), calls=%async_computation.3 | async-start | bytes 1048576
  111.0 628.7 %copy-start.5 = (bf16[1024,32]{0,1:T(8,128)(2,1)S(1)}, bf16[1024,32]{0,1:T(8,128)(2,1)}, u32[]{:S(2)}) copy-start(bf16[1024,32]{0,1:T(8,128)(2,1)} %param.25) | copy-start | bytes 196612
Sparse Core Ops, SparseCore 0:
  109.9 140.5 all-gather.8
  401.2 256.3 all-reduce.2
where the time goes:
time: 798 us; the launch traced here: 795 us
  blocking collectives  412 us (52%)
  waiting for transfers between devices  255 us (32%)
  other arithmetic  66.5 us (8%)
  local copies, waits for them, and re-layouts  33.7 us (4%)
  between operations  15.6 us (2%)
  matrix products  8.65 us (1%)
    unnamed x3, waiting for transfers between devices  255 us
    all_gather x2, blocking collectives, combined_all(): everything = jax.tree.map(lambda part: lax.all_gather(part, axis), x)  160 us
    all_gather x1, blocking collectives, per_device(): lax.all_gather(query_rows.reshape(home_rows, query_heads * HEAD_SIZE), 'p...  88.2 us
    all_gather x1, blocking collectives, per_device(): lax.all_gather(activation, 'pool', axis=0, tiled=True)  80.6 us
    add x63, other arithmetic, combine(): early_out + late_out  55.6 us
    psum x1, blocking collectives, per_device(): mlp_out = narrow_rows(lax.psum(projected_down, 'kv'))  23.6 us
    all_to_all x1, blocking collectives, per_device(): lax.all_to_all(mlp_in, 'pool', split_axis=1, concat_axis=0, tiled=True)  23.6 us
    all_to_all x1, blocking collectives, per_device(): lax.all_to_all(mlp_out, 'pool', split_axis=0, concat_axis=1, tiled=True)  23.4 us
  transfers between devices with their start and end apart: 2, of which 1 were waited for; matrix products, arithmetic and copies ran while one was open for 1% of the time, Pallas kernels for 0%

commit v1 on v0

--- a/solution.py
+++ b/solution.py
@@ -157,7 +157,9 @@
     )
     activation = narrow_rows(jax.nn.silu(summed[:, :hidden_width]) * summed[:, hidden_width:])
     projected_down = jnp.dot(
-        lax.all_gather(activation, "pool", axis=0, tiled=True),
+        jnp.concatenate(
+            lax.all_to_all(jnp.stack([activation] * lax.axis_size("pool")), "pool", 0, 0), axis=0
+        ),
         w_down,
         preferred_element_type=jnp.float32,
     )

time: 798 us -> 740 us (0.927)
  blocking collectives: 412 us -> 352 us
    all_gather x1 -> x0, blocking collectives: 80.6 us -> none  [per_device(): lax.all_gather(activation, 'pool', axis=0, tiled=True)]
    all_to_all x0 -> x1, blocking collectives: none -> 23.9 us  [per_device(): lax.all_to_all(jnp.stack([activation] * lax.axis_size('pool')), 'pool', 0...]
where the time goes in v1:
time: 740 us; the launch traced here: 737 us
  blocking collectives  352 us (48%)
  waiting for transfers between devices  255 us (34%)
  other arithmetic  67.9 us (9%)
  local copies, waits for them, and re-layouts  34.6 us (5%)
  between operations  15.6 us (2%)
  matrix products  8.64 us (1%)
    unnamed x3, waiting for transfers between devices  255 us
    all_gather x2, blocking collectives, combined_all(): everything = jax.tree.map(lambda part: lax.all_gather(part, axis), x)  160 us
    all_gather x1, blocking collectives, per_device(): lax.all_gather(query_rows.reshape(home_rows, query_heads * HEAD_SIZE), 'p...  88.2 us
    add x63, other arithmetic, combine(): early_out + late_out  55.6 us
    all_to_all x1, blocking collectives, per_device(): lax.all_to_all(jnp.stack([activation] * lax.axis_size('pool')), 'pool', 0...  23.9 us
    psum x1, blocking collectives, per_device(): mlp_out = narrow_rows(lax.psum(projected_down, 'kv'))  23.6 us
    all_to_all x1, blocking collectives, per_device(): lax.all_to_all(mlp_in, 'pool', split_axis=1, concat_axis=0, tiled=True)  23.6 us
    all_to_all x1, blocking collectives, per_device(): lax.all_to_all(mlp_out, 'pool', split_axis=0, concat_axis=1, tiled=True)  19.8 us
  transfers between devices with their start and end apart: 2, of which 1 were waited for; matrix products, arithmetic and copies ran while one was open for 1% of the time, Pallas kernels for 0%

profile of v1, /device:TPU:8, one launch (start us, length us, event | category | flops | bytes accessed | tf_op | source)
XLA Modules:
  0.0 736.6 jit_solution(7008568991899991825)
XLA Ops:
  8.0 1.2 dynamic_slice.42
  10.6 1.3 multiply_reduce_fusion.1
  13.3 1.5 fusion.5
  15.0 88.2 %all-gather.3 = bf16[64,1,256]{2,1,0:T(2,128)(2,1)S(1)} all-gather(bf16[1,1,256]{2,1,0:T(2,128)(2,1)S(1)} %reshape.625), channel_id=1, replica_groups=mesh['kv'=8,'pool'=64] {'pool'}, dimensions={0}, use_global_device_ids=true | all-gather | bytes 33280 | tf_op jit(solution)/shard_map/all_gather | solution.py:85
  103.4 1.3 gather_fusion
  105.5 1.5 fusion.61
  107.5 1.3 fusion.10
  108.8 0.9 fusion.20
  109.8 1.2 convolution_bitcast_fusion.2
  111.2 1.2 fusion.4
  112.6 79.4 %all-gather.5 = f32[64,64,2]{1,2,0:T(2,128)S(1)} all-gather(f32[1,64,2]{1,2,0:T(2,128)S(1)} %convolution_bitcast_fusion), channel_id=3, replica_groups=mesh['kv'=8,'pool'=64] {'pool'}, dimensions={0}, use_global_device_ids=true | all-gather | bytes 33280 | tf_op jit(solution)/shard_map/all_gather | solution.py:16
  192.2 81.0 %all-gather.4 = f32[64,64,2]{1,2,0:T(2,128)S(1)} all-gather(f32[1,64,2]{1,2,0:T(2,128)S(1)} %bitcast.154), channel_id=2, replica_groups=mesh['kv'=8,'pool'=64] {'pool'}, dimensions={0}, use_global_device_ids=true | all-gather | bytes 33280 | tf_op jit(solution)/shard_map/all_gather | solution.py:16
  274.2 87.2 %while.19 = (s32[]{:T(128)}, f32[64,2]{0,1:T(2,128)S(1)}, f32[64,2]{0,1:T(2,128)S(1)}, f32[64,256]{1,0:T(8,128)S(1)}, f32[64,64,2]{1,2,0:T(2,128)S(1)}, /*index=...) while((s32[]{:T(128)}, f32[64,2]{0,1:T(2,128)S(1)}, ...), condition=%wide.region_6.7_spmd, body=%wide.region_5.6_spmd.sunk | while | flops 49925 | bytes 466071 | solution.py:22
  277.5 0.9 fusion.74
  278.8 0.9 fusion.74
  280.2 0.9 fusion.74
  281.6 0.9 fusion.74
  287.1 0.9 fusion.74
  288.5 0.9 fusion.74
  289.9 0.9 fusion.74
  295.5 0.9 fusion.74
  296.8 0.9 fusion.74
  298.2 0.9 fusion.74
  362.0 12.6 %psum.14 = f32[1,2048]{1,0:T(1,128)S(1)} all-reduce(f32[1,2048]{1,0:T(1,128)S(1)} %fusion.62), channel_id=1, replica_groups=mesh['kv'=8,'pool'=64] {'kv'}, use_global_device_ids=true, to_apply=%region_8.9 | all-reduce | flops 2048 | bytes 16384 | tf_op jit(solution)/shard_map/psum | solution.py:148
  376.2 23.6 %all_to_all.35 = bf16[1,64,32]{2,0,1:T(2,128)(2,1)S(1)} all-to-all(bf16[1,64,32]{2,0,1:T(2,128)(2,1)S(1)} %all_to_all.31), channel_id=1, replica_groups=mesh['kv'=8,'pool'=64] {'pool'}, dimensions={1} | all-to-all | bytes 8192 | tf_op jit(solution)/shard_map/all_to_all | solution.py:151
  401.1 1.3 dynamic-slice
  402.4 255.3 %all-reduce.3.cloned.1.call-done = f32[64,2048]{1,0:T(8,128)} async-done(((f32[64,2048]{1,0:T(8,128)}), f32[64,2048]{1,0:T(8,128)}) %all-reduce.3.cloned.1.call-update) | async-done | bytes 524304
  657.7 1.5 fusion.39
  659.9 1.4 reduce.17
  661.3 23.9 %all_to_all.36 = bf16[64,2,512]{2,1,0:T(2,128)(2,1)S(1)} all-to-all(bf16[64,2,512]{2,1,0:T(2,128)(2,1)S(1)} %reshape.659), channel_id=1, replica_groups=mesh['kv'=8,'pool'=64] {'pool'}, dimensions={0} | all-to-all | bytes 262144 | tf_op jit(solution)/shard_map/all_to_all | solution.py:161
  685.5 23.6 %psum.15 = bf16[64,32]{0,1:T(8,128)(2,1)S(1)} all-reduce(f32[64,32]{0,1:T(8,128)S(1)} %fusion.17), channel_id=1, replica_groups=mesh['kv'=8,'pool'=64] {'kv'}, use_global_device_ids=true, to_apply=%region_11.12 | all-reduce | flops 2048 | bytes 12288 | tf_op jit(solution)/shard_map/psum | solution.py:166
  709.2 19.8 %all_to_all.37 = bf16[64,1,32]{2,1,0:T(2,128)(2,1)S(1)} all-to-all(bf16[64,1,32]{2,1,0:T(2,128)(2,1)S(1)} %copy.51), channel_id=1, replica_groups=mesh['kv'=8,'pool'=64] {'pool'}, dimensions={0} | all-to-all | bytes 8192 | tf_op jit(solution)/shard_map/all_to_all | solution.py:167
  (441 shorter events, 86.7 us)
Async XLA Ops:
  6.5 355.2 %copy-start = (bf16[256,2048]{1,0:T(8,128)(2,1)S(1)}, bf16[256,2048]{1,0:T(8,128)(2,1)}, u32[]{:S(2)}) copy-start(bf16[256,2048]{1,0:T(8,128)(2,1)} %param.18) | copy-start | bytes 3145732
  6.5 105.9 %copy-start.4 = (bf16[2048]{0:T(1024)(128)(2,1)S(1)}, bf16[2048]{0:T(1024)(128)(2,1)}, u32[]{:S(2)}) copy-start(bf16[2048]{0:T(1024)(128)(2,1)} %param.22) | copy-start | bytes 12292
  6.5 266.8 %all-gather.8.cloned.1.call-start = ((), (), s32[]{:S(2)}) async-start(), calls=%async_computation.3 | async-start | bytes 4259840 | tf_op jit(solution)/shard_map/all_gather | solution.py:16
  14.8 359.9 %copy-start.1 = (bf16[1,2048]{1,0:T(2,128)(2,1)S(1)}, bf16[1,2048]{1,0:T(2,128)(2,1)}, u32[]{:S(2)}) copy-start(bf16[1,2048]{1,0:T(2,128)(2,1)} %param.14) | copy-start | bytes 12292
  15.0 384.8 %copy-start.2 = (bf16[32,1024]{1,0:T(8,128)(2,1)S(1)}, bf16[32,1024]{1,0:T(8,128)(2,1)}, u32[]{:S(2)}) copy-start(bf16[32,1024]{1,0:T(8,128)(2,1)} %param.24) | copy-start | bytes 196612
  103.4 296.6 %copy-start.3 = (bf16[32,1024]{1,0:T(8,128)(2,1)S(1)}, bf16[32,1024]{1,0:T(8,128)(2,1)}, u32[]{:S(2)}) copy-start(bf16[32,1024]{1,0:T(8,128)(2,1)} %param.23) | copy-start | bytes 196612
  109.7 547.9 %all-reduce.3.cloned.1.call-start = ((), (), s32[]{:S(2)}) async-start(), calls=%async_computation.4 | async-start | bytes 1048576
  274.2 411.1 %copy-start.5 = (bf16[1024,32]{0,1:T(8,128)(2,1)S(1)}, bf16[1024,32]{0,1:T(8,128)(2,1)}, u32[]{:S(2)}) copy-start(bf16[1024,32]{0,1:T(8,128)(2,1)} %param.25) | copy-start | bytes 196612
Sparse Core Ops, SparseCore 0:
  109.9 140.5 all-gather.7
  401.2 256.3 all-reduce.2
